TPU v7x, 512 devices: a whole 4x4x16 slice. The times are simulated.
512 devices in a mesh: rowpt: 32 (over y, z_hi, core), colpt: 16 (over z_lo, x).
Axes of the slice: x: 4, y: 4, z: 16 (z_hi: 4, z_lo: 4; z = z_hi * 4 + z_lo), core: 2. Of those that a mesh axis runs over, the one named last changes fastest.
Arguments:
- x_pairs: float32 [4, 1024, 1024], P(None, 'rowpt', 'colpt'), may hold values from -6 to 6
- eps_val: float32 [1024], P('rowpt'), may hold values from -2 to -0.5
- eps_con: float32 [1024], P('colpt'), may hold values from 0.5 to 2
- orb_val: float32 [8192, 1024], P(('rowpt', 'colpt')), may hold values from -0.35 to 0.35
- orb_con: float32 [8192, 1024], P(('rowpt', 'colpt')), may hold values from -0.35 to 0.35
- screened_w: float32 [8192, 8192], P('rowpt', 'colpt'), may hold values from -0.0625 to 0.0625
Outputs:
- hx: float32 [4, 1024, 1024], P(None, 'rowpt', 'colpt')
All inputs are finite; a program needn't handle non-finite values.
Results may differ from a plain program's by a relative error of at most 0.00005.
Values sent between devices are 32-bit elements; how exact they have to be, the bound alone decides.
A program may use at most 64 MiB of HBM per device.

v0:
```python
import jax
import jax.numpy as jnp
from jax import lax
from jax.sharding import PartitionSpec as P

NP = 8192


def joined_along(pieces, dim):
    lengths = list(pieces.shape[1:])
    lengths[dim] *= pieces.shape[0]
    return jnp.moveaxis(pieces, 0, dim).reshape(lengths)


def copy_for_each(array, axis):
    copies = jnp.broadcast_to(array, (lax.axis_size(axis), *array.shape))
    return lax.all_to_all(copies, axis, split_axis=0, concat_axis=0, tiled=True)


def gathered_copies(array, axis, dim):
    return joined_along(copy_for_each(array, axis), dim)


def in_blocks(array, dim, devices):
    lengths = array.shape
    pieces = array.reshape(*lengths[:dim], devices, lengths[dim] // devices, *lengths[dim + 1 :])
    return jnp.moveaxis(pieces, dim, 0)


def sent_and_summed(array, axis, dim):
    devices = lax.axis_size(axis)
    pieces = lax.all_to_all(in_blocks(array, dim, devices), axis, 0, 0, tiled=True)
    return jnp.sum(pieces, axis=0)


def over_copies(array, axis):
    everything = copy_for_each(array, axis)
    return jnp.sum(everything, axis=0)


def reorder_points(values, outer, inner):
    width = values.shape[1]
    shaped = values.reshape(outer, inner, -1, width)
    return jnp.transpose(shaped, (1, 0, 2, 3)).reshape(-1, width)


def per_device(x_pairs, eps_val, eps_con, orb_val, orb_con, screened_w):
    nrow = lax.axis_size("rowpt")
    ncol = lax.axis_size("colpt")
    val_part = lax.all_to_all(orb_val, "rowpt", split_axis=1, concat_axis=0, tiled=True)
    val_mixed = gathered_copies(val_part, "colpt", 0)
    val_cols = reorder_points(val_mixed, ncol, nrow)
    con_part = lax.all_to_all(orb_con, "colpt", split_axis=1, concat_axis=0, tiled=True)
    con_cols = lax.all_gather(con_part, "rowpt", axis=0, tiled=True)
    block_pts = min(NP, 2048)
    nblocks = NP // block_pts
    vecs = x_pairs.shape[0]
    val_blocks = val_cols.reshape(nblocks, block_pts, val_cols.shape[1])
    con_blocks = con_cols.reshape(nblocks, block_pts, con_cols.shape[1])

    def density_block(pieces):
        val_piece, con_piece = pieces
        through = jnp.einsum("pc,bvc->bpv", con_piece, x_pairs, precision=lax.Precision.HIGHEST)
        return jnp.sum(through * val_piece[None], axis=2)

    partial_density = lax.map(density_block, (val_blocks, con_blocks))
    partial_density = jnp.transpose(partial_density, (1, 0, 2)).reshape(vecs, NP)
    column_share = sent_and_summed(partial_density, "colpt", 1)
    density = over_copies(column_share, "rowpt")
    screened_part = jnp.einsum("bq,pq->bp", density, screened_w, precision=lax.Precision.HIGHEST)
    row_total = over_copies(screened_part, "colpt")
    screened = gathered_copies(row_total, "rowpt", 1)
    pot_blocks = jnp.transpose(screened.reshape(vecs, nblocks, block_pts), (1, 0, 2))

    def kernel_block(total, pieces):
        val_piece, con_piece, pot_piece = pieces
        weighted = val_piece[None] * pot_piece[:, :, None]
        step = jnp.einsum("bpv,pc->bvc", weighted, con_piece, precision=lax.Precision.HIGHEST)
        return (total + step, None)

    start = jnp.zeros(x_pairs.shape, jnp.float32)
    kernel, unused = lax.scan(kernel_block, start, (val_blocks, con_blocks, pot_blocks))
    diff = eps_con[None, None, :] - eps_val[None, :, None]
    return diff * x_pairs + kernel


def solution(mesh):
    in_specs = (
        P(None, "rowpt", "colpt"),
        P("rowpt"),
        P("colpt"),
        P(("rowpt", "colpt"), None),
        P(("rowpt", "colpt"), None),
        P("rowpt", "colpt"),
    )
    out_specs = P(None, "rowpt", "colpt")
    return jax.shard_map(
        per_device, mesh=mesh, in_specs=in_specs, out_specs=out_specs, check_vma=False
    )
```

profile of v0, /device:TPU:1, one launch (start us, length us, event | category | flops | bytes accessed | tf_op | source)
XLA Modules:
  0.0 251.6 jit_solution(8417644518098035840)
XLA Ops:
  6.5 1.0 all_to_all.48
  7.6 0.8 reshape.48
  8.3 9.0 %all-to-all-start.2 = ((f32[16,1,1024]{2,1,0:T(1,128)}), f32[16,1,1024]{2,1,0:T(1,128)S(1)}, u32[]{:S(2)}, u32[]{:S(2)}) async-start(f32[16,1,1024]{2,1,0:T(1,128)} %reshape.48), calls=%async_computation.2 | async-start | bytes 131072 | tf_op jit(solution)/shard_map/all_to_all | solution.py:53
  17.3 1.0 all_to_all.43
  18.3 0.2 copy.69
  18.5 0.8 reshape.46
  19.3 5.3 %all-to-all-done.2 = f32[16,1,1024]{2,1,0:T(1,128)S(1)} async-done(((f32[16,1,1024]{2,1,0:T(1,128)}), f32[16,1,1024]{2,1,0:T(1,128)S(1)}, u32[]{:S(2)}, u32[]{:S(2)}) %all-to-all-start.2) | async-done | bytes 65568 | tf_op jit(solution)/shard_map/all_to_all | solution.py:53
  24.6 17.3 %all-to-all-start = ((f32[32,1,512]{2,1,0:T(1,128)}), f32[32,1,512]{2,1,0:T(1,128)S(1)}, u32[]{:S(2)}, u32[]{:S(2)}) async-start(f32[32,1,512]{2,1,0:T(1,128)} %reshape.46), calls=%async_computation | async-start | bytes 131072 | tf_op jit(solution)/shard_map/all_to_all | solution.py:50
  41.9 0.5 broadcast.30
  42.4 0.8 reduce.2
  43.3 0.7 reshape.49
  44.0 12.4 %all-to-all-done = f32[32,1,512]{2,1,0:T(1,128)S(1)} async-done(((f32[32,1,512]{2,1,0:T(1,128)}), f32[32,1,512]{2,1,0:T(1,128)S(1)}, u32[]{:S(2)}, u32[]{:S(2)}) %all-to-all-start) | async-done | bytes 65568 | tf_op jit(solution)/shard_map/all_to_all | solution.py:50
  56.4 0.8 reduce.1
  57.2 0.1 reshape.47
  57.5 1.1 broadcast_in_dim.28
  58.6 3.8 %all-to-all-start.1 = ((f32[16,512,32]{1,2,0:T(8,128)}), f32[16,512,32]{1,2,0:T(8,128)S(1)}, u32[]{:S(2)}, u32[]{:S(2)}) async-start(f32[16,512,32]{1,2,0:T(8,128)} %broadcast_in_dim.28), calls=%async_computation.1 | async-start | bytes 2097152 | tf_op jit(solution)/shard_map/all_to_all | solution.py:17
  62.3 32.1 %all-to-all-done.1 = f32[16,512,32]{1,2,0:T(8,128)S(1)} async-done(((f32[16,512,32]{1,2,0:T(8,128)}), f32[16,512,32]{1,2,0:T(8,128)S(1)}, u32[]{:S(2)}, u32[]{:S(2)}) %all-to-all-start.1) | async-done | bytes 1048608 | tf_op jit(solution)/shard_map/all_to_all | solution.py:17
  94.4 2.7 %copy.50 = f32[16,512,32]{2,1,0:T(8,128)} copy(f32[16,512,32]{1,2,0:T(8,128)S(1)} %all-to-all-done.1) | data formatting | bytes 2097152 | tf_op jit(solution)/shard_map/all_to_all | solution.py:17
  97.1 4.7 %copy.51 = f32[32,16,16,32]{3,2,1,0:T(8,128)} copy(f32[32,16,16,32]{3,2,0,1:T(8,128)} %bitcast.61) | data formatting | bytes 2097152 | tf_op jit(solution)/shard_map/transpose | solution.py:44
  101.8 4.0 %copy.60 = f32[4,2048,32]{1,2,0:T(8,128)} copy(f32[4,2048,32]{2,1,0:T(8,128)} %bitcast.62) | data formatting | bytes 2097152
  105.8 42.1 %all-gather.2.cloned.1.call-done = f32[8192,64]{1,0:T(8,128)} async-done(((f32[256,64]{1,0:T(8,128)}), f32[8192,64]{1,0:T(8,128)}) %all-gather.2.cloned.1.call-update) | async-done | bytes 2097168 | tf_op jit(solution)/shard_map/all_gather | solution.py:54
  148.0 2.9 %copy.54 = f32[4,2048,64]{1,2,0:T(8,128)S(1)} copy(f32[4,2048,64]{2,1,0:T(8,128)} %bitcast.63) | data formatting | bytes 4194304 | tf_op jit(solution)/shard_map/while | solution.py:66
  150.8 8.2 %while.21 = (s32[]{:T(128)}, f32[4,4,2048]{2,1,0:T(4,128)S(1)}, f32[4,2048,64]{1,2,0:T(8,128)S(1)}, f32[4,32,64]{2,1,0:T(8,128)S(1)}, f32[4,2048,32]{1,2,0:T(8,128)}, /*index=5*/s32[]{:T(128)}) while((s32[]{:T(128)}, f32[4,4,2048]{2,1,0:T(4,128)S(1)}, f32[4,2048,64]{1,2,0:T(8,128)S(1)}, f32[4,32,64]{2,1,0:T(8,128)S(1)}, ...), condition=%wide.region_2.3_spmd, body=%wide.region_0.2_spmd.sunk | while | flops 201842688 | bytes 1474641 | solution.py:66
  150.9 1.0 dynamic-slice_bitcast_fusion.6
  151.8 1.0 fusion.21
  152.9 1.0 dynamic-slice_bitcast_fusion.6
  153.9 1.0 fusion.21
  155.0 1.0 dynamic-slice_bitcast_fusion.6
  156.0 1.0 fusion.21
  157.0 1.0 dynamic-slice_bitcast_fusion.6
  158.0 1.0 fusion.21
  159.4 13.3 %all_to_all.63 = f32[16,4,512]{2,1,0:T(4,128)S(1)} all-to-all(f32[16,4,512]{2,1,0:T(4,128)S(1)} %copy.57), channel_id=1, replica_groups=mesh['rowpt'=32,'colpt'=16] {'colpt'}, dimensions={0} | all-to-all | bytes 262144 | tf_op jit(solution)/shard_map/all_to_all | solution.py:32
  172.7 28.1 %all_to_all.64 = f32[32,4,512]{2,1,0:T(4,128)S(1)} all-to-all(f32[32,4,512]{2,1,0:T(4,128)S(1)} %broadcast_in_dim.30), channel_id=1, replica_groups=mesh['rowpt'=32,'colpt'=16] {'rowpt'}, dimensions={0} | all-to-all | bytes 524288 | tf_op jit(solution)/shard_map/all_to_all | solution.py:17
  200.9 0.5 fusion.10
  201.4 12.9 %all_to_all.65 = f32[16,4,256]{2,1,0:T(4,128)S(1)} all-to-all(f32[16,4,256]{2,1,0:T(4,128)S(1)} %broadcast_in_dim.31), channel_id=1, replica_groups=mesh['rowpt'=32,'colpt'=16] {'colpt'}, dimensions={0} | all-to-all | bytes 131072 | tf_op jit(solution)/shard_map/all_to_all | solution.py:17
  214.4 0.7 broadcast_in_dim.32
  215.0 5.4 %all-to-all-start.6 = ((f32[32,4,256]{2,1,0:T(4,128)}), f32[32,4,256]{2,1,0:T(4,128)S(1)}, u32[]{:S(2)}, u32[]{:S(2)}) async-start(f32[32,4,256]{2,1,0:T(4,128)} %broadcast_in_dim.32), calls=%async_computation.6 | async-start | bytes 262144 | tf_op jit(solution)/shard_map/all_to_all | solution.py:17
  220.6 15.5 %all-to-all-done.6 = f32[32,4,256]{2,1,0:T(4,128)S(1)} async-done(((f32[32,4,256]{2,1,0:T(4,128)}), f32[32,4,256]{2,1,0:T(4,128)S(1)}, u32[]{:S(2)}, u32[]{:S(2)}) %all-to-all-start.6) | async-done | bytes 131104 | tf_op jit(solution)/shard_map/all_to_all | solution.py:17
  236.0 8.0 %while.22 = (s32[]{:T(128)}, f32[4,32,64]{2,1,0:T(8,128)S(1)}, f32[4,2048,32]{1,2,0:T(8,128)}, f32[4,4,2048]{2,1,0:T(4,128)S(1)}, f32[4,2048,64]{1,2,0:T(8,128)S(1)}, /*index=5*/s32[]{:T(128)}, s32[]{:T(128)}) while((s32[]{:T(128)}, f32[4,32,64]{2,1,0:T(8,128)S(1)}, f32[4,2048,32]{1,2,0:T(8,128)}, f32[4,4,2048]{2,1,0:T(4,128)S(1)}, ...), condition=%wide.region_7.8_spmd.clone, body=%wide.region_6.7_spmd.clone.sunk | while | flops 201605120 | bytes 1507427 | solution.py:82
  236.0 1.0 dynamic-slice_bitcast_fusion.8
  237.0 1.0 convolution_add_fusion.2
  238.1 1.0 dynamic-slice_bitcast_fusion.8
  239.1 1.0 convolution_add_fusion.2
  240.1 1.0 dynamic-slice_bitcast_fusion.8
  241.1 1.0 convolution_add_fusion.2
  242.1 1.0 dynamic-slice_bitcast_fusion.8
  243.1 1.0 convolution_add_fusion.2
  244.1 0.6 multiply_add_fusion
  (31 shorter events, 0.8 us)
Async XLA Ops:
  6.5 194.3 %copy-start = (f32[256,512]{1,0:T(8,128)S(1)}, f32[256,512]{1,0:T(8,128)}, u32[]{:S(2)}) copy-start(f32[256,512]{1,0:T(8,128)} %param.15) | copy-start | bytes 1572868
  8.3 16.3 %all-to-all-start.2 = ((f32[16,1,1024]{2,1,0:T(1,128)}), f32[16,1,1024]{2,1,0:T(1,128)S(1)}, u32[]{:S(2)}, u32[]{:S(2)}) async-start(f32[16,1,1024]{2,1,0:T(1,128)} %reshape.48), calls=%async_computation.2 | async-start | bytes 131072 | tf_op jit(solution)/shard_map/all_to_all | solution.py:53
  24.6 31.8 %all-to-all-start = ((f32[32,1,512]{2,1,0:T(1,128)}), f32[32,1,512]{2,1,0:T(1,128)S(1)}, u32[]{:S(2)}, u32[]{:S(2)}) async-start(f32[32,1,512]{2,1,0:T(1,128)} %reshape.46), calls=%async_computation | async-start | bytes 131072 | tf_op jit(solution)/shard_map/all_to_all | solution.py:50
  41.9 106.1 %all-gather.2.cloned.1.call-start = ((), (), s32[]{:S(2)}) async-start(), calls=%async_computation.7 | async-start | bytes 4325376 | tf_op jit(solution)/shard_map/all_gather | solution.py:54
  58.6 35.8 %all-to-all-start.1 = ((f32[16,512,32]{1,2,0:T(8,128)}), f32[16,512,32]{1,2,0:T(8,128)S(1)}, u32[]{:S(2)}, u32[]{:S(2)}) async-start(f32[16,512,32]{1,2,0:T(8,128)} %broadcast_in_dim.28), calls=%async_computation.1 | async-start | bytes 2097152 | tf_op jit(solution)/shard_map/all_to_all | solution.py:17
  148.0 2.9 %copy-start.1 = (f32[4,32,64]{2,1,0:T(8,128)S(1)}, f32[4,32,64]{2,1,0:T(8,128)}, u32[]{:S(2)}) copy-start(f32[4,32,64]{2,1,0:T(8,128)} %param.10) | copy-start | bytes 98308
  159.1 61.4 %copy-start.2 = (f32[32]{0:T(128)S(1)}, f32[32]{0:T(128)}, u32[]{:S(2)}) copy-start(f32[32]{0:T(128)} %param.11) | copy-start | bytes 388
  159.1 61.4 %copy-start.3 = (f32[64]{0:T(128)S(1)}, f32[64]{0:T(128)}, u32[]{:S(2)}) copy-start(f32[64]{0:T(128)} %param.12) | copy-start | bytes 772
  215.0 21.0 %all-to-all-start.6 = ((f32[32,4,256]{2,1,0:T(4,128)}), f32[32,4,256]{2,1,0:T(4,128)S(1)}, u32[]{:S(2)}, u32[]{:S(2)}) async-start(f32[32,4,256]{2,1,0:T(4,128)} %broadcast_in_dim.32), calls=%async_computation.6 | async-start | bytes 262144 | tf_op jit(solution)/shard_map/all_to_all | solution.py:17
Sparse Core Ops, SparseCore 0:
  45.8 102.0 all-gather.1
where the time goes:
time: 253 us; the launch traced here: 252 us
  waiting for transfers between devices  107 us (42%)
  blocking collectives  54.3 us (21%)
  starting transfers between devices  35.5 us (14%)
  local copies, waits for them, and re-layouts  29.4 us (12%)
  between operations  13.6 us (5%)
  matrix products  8.63 us (3%)
    all_to_all x2, waiting for transfers between devices, copy_for_each(): return lax.all_to_all(copies, axis, split_axis=0, concat_axis=0, tiled=True)  47.5 us
    all_gather x1, waiting for transfers between devices, per_device(): con_cols = lax.all_gather(con_part, 'rowpt', axis=0, tiled=True)  42.1 us
    all_to_all x2, blocking collectives, copy_for_each(): return lax.all_to_all(copies, axis, split_axis=0, concat_axis=0, tiled=True)  41 us
    all_to_all x1, starting transfers between devices, per_device(): lax.all_to_all(orb_val, 'rowpt', split_axis=1, concat_axis=0, tiled=True)  17.3 us
    all_to_all x1, blocking collectives, sent_and_summed(): lax.all_to_all(in_blocks(array, dim, devices), axis, 0, 0, tiled=True)  13.3 us
    all_to_all x1, waiting for transfers between devices, per_device(): lax.all_to_all(orb_val, 'rowpt', split_axis=1, concat_axis=0, tiled=True)  12.4 us
    all_to_all x2, starting transfers between devices, copy_for_each(): return lax.all_to_all(copies, axis, split_axis=0, concat_axis=0, tiled=True)  9.2 us
    all_to_all x1, starting transfers between devices, per_device(): lax.all_to_all(orb_con, 'colpt', split_axis=1, concat_axis=0, tiled=True)  9 us
  transfers between devices with their start and end apart: 5, of which 5 were waited for; matrix products, arithmetic and copies ran while one was open for 7% of the time, Pallas kernels for 0%

commit v1 on v0

v1 whole, which is shorter than its diff:
```python
import jax
import jax.numpy as jnp
from jax import lax
from jax.experimental import pallas as pl
from jax.experimental.pallas import tpu as pltpu
from jax.sharding import PartitionSpec as P

MESH = pl.DeviceIdType.MESH
F32 = jnp.float32
BF16 = jnp.bfloat16

V1, C1, V2, C2, XD, DA, DB, DW, SA, SB, KD = range(11)
NSEM = 11


def halves(a):
    hi = a.astype(BF16)
    return hi, (a - hi.astype(F32)).astype(BF16)


def dot_of(a, b, dims):
    return lax.dot_general(a, b, (dims, ((), ())), preferred_element_type=F32)


def dot3(a, b, dims):
    (ah, al), (bh, bl) = a, b
    return dot_of(ah, bh, dims) + (dot_of(ah, bl, dims) + dot_of(al, bh, dims))


NT = ((1,), (1,))
NN = ((1,), (0,))


def kernel(
    x_ref, val_ref, con_ref, w_ref, out_ref,
    xp, xr, v1, c1, vb, cb, vt, ch, cl, wh, wl,
    dpart, da, das, db, dbs, dw, sp, sa, sas, sb, kp, kr,
    rsem, ssem, selfsem,
):
    row = lax.axis_index("rowpt")
    col = lax.axis_index("colpt")
    y, zh, k = row // 8, (row // 2) % 4, row % 2
    zl, x = col // 4, col % 4
    s, h = zl % 2, zl // 2

    def row_of(y_, zh_, k_):
        return y_ * 8 + zh_ * 2 + k_

    def send(src, dst, sem, to_row, to_col):
        pltpu.make_async_remote_copy(
            src_ref=src, dst_ref=dst, send_sem=ssem.at[sem], recv_sem=rsem.at[sem],
            device_id=(to_row, to_col), device_id_type=MESH,
        ).start()

    def keep(src, dst, sem):
        pltpu.make_async_copy(src, dst, rsem.at[sem]).start()

    def arrived(buf, sem):
        pltpu.make_async_copy(buf, buf, rsem.at[sem]).wait()

    def sent(buf, sem):
        pltpu.make_async_copy(buf, buf, ssem.at[sem]).wait()

    def cols(block, width):
        return pl.ds(pl.multiple_of(block * width, width), width)

    for d in range(1, 4):
        to = (y + d) % 4
        send(val_ref.at[:, cols(to, 256)], v1.at[y], V1, row_of(to, zh, k), col)
        to = (x + d) % 4
        send(con_ref.at[:, cols(to, 256)], c1.at[x], C1, row, zl * 4 + to)
    keep(val_ref.at[:, cols(y, 256)], v1.at[y], V1)
    keep(con_ref.at[:, cols(x, 256)], c1.at[x], C1)

    xp[...] = jnp.concatenate([x_ref[:, 0:16, :], x_ref[:, 16:32, :]], axis=2)
    xslot = (zh % 2) * 4 + k * 2 + x % 2
    for a in range(4):
        for b in range(2):
            to_row = row_of(y, (zh + a) % 4, x // 2)
            to_col = (((h + b) % 2) * 2 + zh // 2) * 4 + zl
            if a or b:
                send(xp, xr.at[xslot], XD, to_row, to_col)
            else:
                xself = (to_row == row) & (to_col == col)

                @pl.when(xself)
                def _():
                    keep(xp, xr.at[xslot], XD)

                @pl.when(jnp.logical_not(xself))
                def _():
                    pltpu.make_async_remote_copy(
                        src_ref=xp, dst_ref=xr.at[xslot], send_sem=selfsem.at[0], recv_sem=rsem.at[XD],
                        device_id=(to_row, to_col), device_id_type=MESH,
                    ).start()

    arrived(v1, V1)
    for d in range(1, 16):
        to_x, to_s, to_k = (x + d // 4) % 4, (s + d // 2) % 2, (k + d) % 2
        send(v1.at[:, :, cols(to_s, 128)], vb.at[:, k, s, x], V2, row_of(y, zh, to_k), (h * 2 + to_s) * 4 + to_x)
    keep(v1.at[:, :, cols(s, 128)], vb.at[:, k, s, x], V2)
    arrived(c1, C1)
    for d in range(1, 16):
        to_y, to_s, to_k = (y + d // 4) % 4, (s + d // 2) % 2, (k + d) % 2
        send(c1.at[:, :, cols(to_k, 128)], cb.at[y, k, s], C2, row_of(to_y, zh, to_k), (h * 2 + to_s) * 4 + x)
    keep(c1.at[:, :, cols(k, 128)], cb.at[y, k, s], C2)

    w_hi, w_lo = halves(w_ref[...])
    wh[...] = w_hi
    wl[...] = w_lo

    arrived(xr, XD)
    lane = lax.broadcasted_iota(jnp.int32, (4, 16, 128), 2)
    parts = []
    for v in range(4):
        one, two = xr[v * 2], xr[v * 2 + 1]
        parts.append(jnp.where(lane < 64, one, pltpu.roll(two, 64, 2)))
        parts.append(jnp.where(lane < 64, pltpu.roll(one, 64, 2), two))
    trial = jnp.concatenate([p[:, None] for p in parts], axis=1).reshape(512, 128)
    trial = halves(trial)
    arrived(cb, C2)
    arrived(vb, V2)
    for blk in range(4):
        c_hi, c_lo = halves(cb[blk].reshape(256, 128))
        ch[blk] = c_hi
        cl[blk] = c_lo
        v_t = vb[blk].reshape(256, 128).T
        vt[blk] = v_t
        through = dot3(trial, (c_hi, c_lo), NT).reshape(4, 128, 256)
        dens = jnp.sum(through * v_t[None], axis=1)
        dpart[blk] = jnp.concatenate([dens[:, :128], dens[:, 128:]], axis=0)

    for d in range(1, 8):
        to_x, to_k = (x + d // 2) % 4, (k + d) % 2
        send(dpart.at[to_x], da.at[x * 2 + k], DA, row_of(y, zh, to_k), zl * 4 + to_x)
    keep(dpart.at[x], da.at[x * 2 + k], DA)
    arrived(da, DA)
    das[...] = jnp.sum(da[...], axis=0)
    for d in range(1, 8):
        to_y, to_s = (y + d // 2) % 4, (s + d) % 2
        send(das, db.at[y * 2 + s], DB, row_of(to_y, zh, k), (h * 2 + to_s) * 4 + x)
    keep(das, db.at[y * 2 + s], DB)
    arrived(db, DB)
    dbs[...] = jnp.sum(db[...], axis=0)

    dselves = []
    for e in range(2):
        to_row = row_of(y, s * 2 + e, k)
        to_col = x * 4 + zh
        dself = (to_row == row) & (to_col == col)
        dselves.append(dself)

        @pl.when(dself)
        def _():
            keep(dbs, dw.at[h], DW)

        @pl.when(jnp.logical_not(dself))
        def _():
            pltpu.make_async_remote_copy(
                src_ref=dbs, dst_ref=dw.at[h], send_sem=selfsem.at[1 + e], recv_sem=rsem.at[DW],
                device_id=(to_row, to_col), device_id_type=MESH,
            ).start()
    arrived(dw, DW)
    d0, d1 = dw[0], dw[1]
    dens = jnp.concatenate([d0[0:4], d1[0:4], d0[4:8], d1[4:8]], axis=1)
    dens = jnp.concatenate([dens, dens], axis=0)
    scr = dot3(halves(dens), (wh[...], wl[...]), NT)
    sp[...] = jnp.concatenate([scr[0:4, :128], scr[0:4, 128:]], axis=0)

    for d in range(1, 16):
        send(sp, sa.at[col], SA, row, (col + d) % 16)
    keep(sp, sa.at[col], SA)
    arrived(sa, SA)
    sas[...] = jnp.sum(sa[...], axis=0)
    for d in range(1, 8):
        to_y, to_k = (y + d // 2) % 4, (k + d) % 2
        send(sas, sb.at[y * 2 + k], SB, row_of(to_y, zh, to_k), col)
    keep(sas, sb.at[y * 2 + k], SB)
    arrived(sb, SB)

    acc = jnp.zeros((512, 128), F32)
    for blk in range(4):
        pots = []
        for kk in range(2):
            tile = sb[blk * 2 + kk]
            pots.append(jnp.where(h == 0, tile[0:4], tile[4:8]))
        pot = jnp.concatenate(pots, axis=1)
        weighted = (vt[blk][None] * pot[:, None, :]).reshape(512, 256)
        acc = acc + dot3(halves(weighted), (ch[blk], cl[blk]), NN)
    acc = acc.reshape(4, 8, 16, 128)
    for v in range(4):
        one, two = acc[:, v * 2], acc[:, v * 2 + 1]
        kp[v * 2] = jnp.where(lane < 64, one, pltpu.roll(two, 64, 2))
        kp[v * 2 + 1] = jnp.where(lane < 64, pltpu.roll(one, 64, 2), two)

    group = zh * 2 + h
    for e in range(8):
        slot = (xslot + e) % 8
        to_row = row_of(y, s * 2 + slot // 4, (slot // 2) % 2)
        to_col = x * 4 + k * 2 + slot % 2
        if e:
            send(kp.at[slot], kr.at[group], KD, to_row, to_col)
        else:
            kself = (to_row == row) & (to_col == col)

            @pl.when(kself)
            def _():
                keep(kp.at[slot], kr.at[group], KD)

            @pl.when(jnp.logical_not(kself))
            def _():
                pltpu.make_async_remote_copy(
                    src_ref=kp.at[slot], dst_ref=kr.at[group], send_sem=selfsem.at[3], recv_sem=rsem.at[KD],
                    device_id=(to_row, to_col), device_id_type=MESH,
                ).start()
    arrived(kr, KD)
    total = jnp.sum(kr[...], axis=0)
    out_ref[:, 0:16, :] = total[:, :, :64]
    out_ref[:, 16:32, :] = total[:, :, 64:]

    sent(v1.at[0:3], V1)
    sent(c1.at[0:3], C1)
    sent(vt.at[:, 0:120], V2)
    sent(vt.at[:, 0:120], C2)
    sent(xr.at[0:7], XD)
    sent(da.at[0:7], DA)
    sent(db.at[0:7], DB)
    sent(sa.at[0:15], SA)
    sent(sb.at[0:7], SB)
    sent(kr.at[0:7], KD)

    @pl.when(jnp.logical_not(xself))
    def _():
        pltpu.make_async_copy(xp, xp, selfsem.at[0]).wait()

    for e in range(2):

        @pl.when(jnp.logical_not(dselves[e]))
        def _():
            pltpu.make_async_copy(dbs, dbs, selfsem.at[1 + e]).wait()

    @pl.when(jnp.logical_not(kself))
    def _():
        pltpu.make_async_copy(kr.at[0], kr.at[0], selfsem.at[3]).wait()


def per_device(x_pairs, eps_val, eps_con, orb_val, orb_con, screened_w):
    vmem = pl.BlockSpec(memory_space=pltpu.VMEM)
    kern = pl.pallas_call(
        kernel,
        out_shape=jax.ShapeDtypeStruct((4, 32, 64), F32),
        in_specs=[vmem] * 4,
        out_specs=vmem,
        scratch_shapes=[
            pltpu.VMEM((4, 16, 128), F32),
            pltpu.VMEM((8, 4, 16, 128), F32),
            pltpu.VMEM((4, 16, 256), F32),
            pltpu.VMEM((4, 16, 256), F32),
            pltpu.VMEM((4, 2, 2, 4, 16, 128), F32),
            pltpu.VMEM((4, 2, 2, 4, 16, 128), F32),
            pltpu.VMEM((4, 128, 256), F32),
            pltpu.VMEM((4, 256, 128), BF16),
            pltpu.VMEM((4, 256, 128), BF16),
            pltpu.VMEM((256, 512), BF16),
            pltpu.VMEM((256, 512), BF16),
            pltpu.VMEM((4, 8, 128), F32),
            pltpu.VMEM((8, 8, 128), F32),
            pltpu.VMEM((8, 128), F32),
            pltpu.VMEM((8, 8, 128), F32),
            pltpu.VMEM((8, 128), F32),
            pltpu.VMEM((2, 8, 128), F32),
            pltpu.VMEM((8, 128), F32),
            pltpu.VMEM((16, 8, 128), F32),
            pltpu.VMEM((8, 128), F32),
            pltpu.VMEM((8, 8, 128), F32),
            pltpu.VMEM((8, 4, 16, 128), F32),
            pltpu.VMEM((8, 4, 16, 128), F32),
            pltpu.SemaphoreType.DMA((NSEM,)),
            pltpu.SemaphoreType.DMA((NSEM,)),
            pltpu.SemaphoreType.DMA((4,)),
        ],
        compiler_params=pltpu.CompilerParams(has_side_effects=True),
        name="bse_apply",
    )(x_pairs, orb_val, orb_con, screened_w)
    diff = eps_con[None, None, :] - eps_val[None, :, None]
    return diff * x_pairs + kern


def solution(mesh):
    in_specs = (
        P(None, "rowpt", "colpt"),
        P("rowpt"),
        P("colpt"),
        P(("rowpt", "colpt"), None),
        P(("rowpt", "colpt"), None),
        P("rowpt", "colpt"),
    )
    out_specs = P(None, "rowpt", "colpt")
    return jax.shard_map(
        per_device, mesh=mesh, in_specs=in_specs, out_specs=out_specs, check_vma=False
    )
```

time: 253 us -> 104 us (0.41)
  waiting for transfers between devices: 107 us -> 0 us
  Pallas kernels: 0 us -> 101 us
  blocking collectives: 54.3 us -> 0 us
  starting transfers between devices: 35.5 us -> 0 us
  local copies, waits for them, and re-layouts: 29.4 us -> 0.01 us
  between operations: 13.6 us -> 0.02 us
  matrix products: 8.63 us -> 0 us
    pallas_call x0 -> x1, Pallas kernels: none -> 101 us  [per_device(): pl.pallas_call(kernel, out_shape=jax.ShapeDtypeStruct((4, 32, 64), F32),...]
    all_to_all x4 -> x0, waiting for transfers between devices: 65.3 us -> none  [the longest x2 47.5 us: copy_for_each(): return lax.all_to_all(copies, axis, split_axis=0, concat_axis=0, tiled=True)]
    all_to_all x3 -> x0, blocking collectives: 54.3 us -> none  [the longest x2 41 us: copy_for_each(): return lax.all_to_all(copies, axis, split_axis=0, concat_axis=0, tiled=True)]
    all_gather x1 -> x0, waiting for transfers between devices: 42.1 us -> none  [per_device(): con_cols = lax.all_gather(con_part, 'rowpt', axis=0, tiled=True)]
    all_to_all x4 -> x0, starting transfers between devices: 35.5 us -> none  [the longest x1 17.3 us: per_device(): lax.all_to_all(orb_val, 'rowpt', split_axis=1, concat_axis=0, tiled=True)]
    dot_general x9 -> x0, matrix products: 8.63 us -> none  [the longest x4 4.17 us: density_block(): jnp.einsum('pc,bvc->bpv', con_piece, x_pairs, precision=lax.Precision.HIG...]
    mul x12 -> x0, local copies, waits for them, and re-layouts: 7.82 us -> none  [the longest x8 3.93 us: kernel_block(): weighted = val_piece[None] * pot_piece[:, :, None]]
    unnamed x13 -> x2, local copies, waits for them, and re-layouts: 6.44 us -> 0.01 us
  transfers between devices with their start and end apart: 5 -> 0, of which waited for: 5 -> 0; matrix products, arithmetic and copies ran while one was open for 7% -> 0% of each run, Pallas kernels for 0% -> 0%
where the time goes in v1:
time: 104 us
  Pallas kernels  101 us (97%)
  other arithmetic  2.22 us (2%)
    pallas_call x1, Pallas kernels, per_device(): pl.pallas_call(kernel, out_shape=jax.ShapeDtypeStruct((4, 32, 64), F32),...  101 us

profile of v1, /device:TPU:1, one launch (start us, length us, event | category | flops | bytes accessed | tf_op | source)
XLA Modules:
  0.0 103.6 jit_solution(12183327052996766875)
XLA Ops:
  0.0 0.7 broadcast_subtract_fusion
  0.7 0.0 copy-start
  0.7 101.4 %bse_apply.1 = f32[4,32,64]{2,1,0:T(8,128)} custom-call(f32[4,32,64]{2,1,0:T(8,128)} %x_ref.1, f32[16,1024]{1,0:T(8,128)} %val_ref.1, f32[16,1024]{1,0:T(8,128)} %con_ref.1, f32[256,512]{1,0:T(8,128)} %w_ref.1), custom_call_target="tpu_custom_call" | custom-call | tf_op jit(solution)/shard_map/bse_apply/pallas_call | solution.py:249
  102.1 0.0 copy-done
  102.1 1.5 %multiply_add_fusion = f32[4,32,64]{2,1,0:T(8,128)} fusion(f32[4,32,64]{2,1,0:T(8,128)} %bse_apply.1, f32[4,32,64]{2,1,0:T(8,128)S(1)} %copy-done, f32[32,64]{1,0:T(8,128)S(1)} %broadcast_subtract_fusion), kind=kLoop, calls=%fused_computation | loop fusion | flops 16384 | bytes 106496 | tf_op jit(solution)/shard_map/add | solution.py:286
Async XLA Ops:
  0.7 101.4 %copy-start = (f32[4,32,64]{2,1,0:T(8,128)S(1)}, f32[4,32,64]{2,1,0:T(8,128)}, u32[]{:S(2)}) copy-start(f32[4,32,64]{2,1,0:T(8,128)} %x_ref.1) | copy-start | bytes 98308

commit v2 on v1

v2 whole, which is shorter than its diff:
```python
import jax
import jax.numpy as jnp
from jax import lax
from jax.experimental import pallas as pl
from jax.experimental.pallas import tpu as pltpu
from jax.sharding import PartitionSpec as P

MESH = pl.DeviceIdType.MESH
F32 = jnp.float32
BF16 = jnp.bfloat16

V1, C1, CZ, V2, C2, DA, DB, DW, SA, SB, KD = range(11)
NSEM = 11


def halves(a):
    hi = a.astype(BF16)
    return hi, (a - hi.astype(F32)).astype(BF16)


def dot_of(a, b, dims):
    return lax.dot_general(a, b, (dims, ((), ())), preferred_element_type=F32)


def dot3(a, b, dims):
    (ah, al), (bh, bl) = a, b
    return dot_of(ah, bh, dims) + (dot_of(ah, bl, dims) + dot_of(al, bh, dims))


NT = ((1,), (1,))
NN = ((1,), (0,))


def kernel(
    x_ref, val_ref, con_ref, w_ref, out_ref,
    xp, xr, v1, c1, vb, cb, vt, ch, cl, wh, wl,
    dpart, da, das, db, dbs, dw, sp, sa, sas, sb, kp, kr,
    rsem, ssem, selfsem, xsem, xout,
):
    row = lax.axis_index("rowpt")
    col = lax.axis_index("colpt")
    y, zh, k = row // 8, (row // 2) % 4, row % 2
    zl, x = col // 4, col % 4
    s, h = zl % 2, zl // 2

    def row_of(y_, zh_, k_):
        return y_ * 8 + zh_ * 2 + k_

    def send(src, dst, sem, to_row, to_col):
        pltpu.make_async_remote_copy(
            src_ref=src, dst_ref=dst, send_sem=ssem.at[sem], recv_sem=rsem.at[sem],
            device_id=(to_row, to_col), device_id_type=MESH,
        ).start()

    def keep(src, dst, sem):
        pltpu.make_async_copy(src, dst, rsem.at[sem]).start()

    def arrived(buf, sem):
        pltpu.make_async_copy(buf, buf, rsem.at[sem]).wait()

    leaving = []

    def sent(buf, sem, only=None):
        def wait():
            pltpu.make_async_copy(buf, buf, sem).wait()

        leaving.append(wait if only is None else lambda: pl.when(only)(wait))

    def cols(block, width):
        return pl.ds(pl.multiple_of(block * width, width), width)

    def send_or_keep(src, dst, sem, own_sem, to):
        same = (to[0] == row) & (to[1] == col)

        @pl.when(same)
        def _():
            pltpu.make_async_copy(src, dst, sem).start()

        @pl.when(jnp.logical_not(same))
        def _():
            pltpu.make_async_remote_copy(
                src_ref=src, dst_ref=dst, send_sem=own_sem, recv_sem=sem,
                device_id=to, device_id_type=MESH,
            ).start()

        sent(src, own_sem, jnp.logical_not(same))

    xslot = (zh % 2) * 4 + k * 2 + x % 2

    def ring_peer(d):
        to = (zh * 2 + h + d) % 8
        return row_of(y, to // 2, k), ((to % 2) * 2 + s) * 4 + x

    def pair_peer(slot):
        return row_of(y, s * 2 + slot // 4, (slot // 2) % 2), x * 4 + k * 2 + slot % 2

    def density_peer(e):
        return row_of(y, s * 2 + e, k), x * 4 + zh

    near = []
    for d in range(1, 16):
        near.append((row_of(y, zh, (k + d) % 2), (h * 2 + (s + d // 2) % 2) * 4 + (x + d // 4) % 4))
    for d in range(4, 16):
        near.append((row_of((y + d // 4) % 4, zh, (k + d) % 2), (h * 2 + (s + d // 2) % 2) * 4 + x))
    for d in range(8):
        near.append((row, ((1 - h) * 2 + d // 4) * 4 + d % 4))
    near += [ring_peer(1), ring_peer(-1)]
    barrier = pltpu.get_barrier_semaphore()
    for to in near:
        pl.semaphore_signal(barrier, inc=1, device_id=to, device_id_type=MESH)
    pl.semaphore_wait(barrier, len(near))

    xp[...] = jnp.concatenate([x_ref[:, 0:16, :], x_ref[:, 16:32, :]], axis=2)
    send_or_keep(
        xp, xr.at[xslot], xsem.at[xslot], selfsem.at[0],
        (row_of(y, zh, x // 2), (h * 2 + zh // 2) * 4 + zl),
    )

    def way_of(q):
        return (zh * 2 + h - 4 * s - 2 * q - x // 2 + 16) % 8

    def hand_on(q):
        way = way_of(q)
        for j in range(4):
            piece = xr.at[q * 4 + j]
            pltpu.make_async_copy(piece, piece, xsem.at[q * 4 + j]).wait()
            for on, going in enumerate((way <= 3, (way == 0) | (way >= 6))):
                out = xout.at[on, q * 4 + j]

                @pl.when(going)
                def _():
                    pltpu.make_async_remote_copy(
                        src_ref=piece, dst_ref=piece, send_sem=out, recv_sem=xsem.at[q * 4 + j],
                        device_id=ring_peer(1 - 2 * on), device_id_type=MESH,
                    ).start()

    for q in range(2):
        for on, going in enumerate((way_of(q) <= 3, (way_of(q) == 0) | (way_of(q) >= 6))):
            for j in range(4):
                sent(xp, xout.at[on, q * 4 + j], going)

    def steps_of(q):
        way = way_of(q)
        return jnp.minimum(way, 8 - way)

    first = jnp.where(steps_of(0) <= steps_of(1), 0, 1)
    at_start = way_of(first) == 0

    for d in range(1, 8):
        to_x, to_k = (x + d // 2) % 4, (k + d) % 2
        send(con_ref.at[:, cols(to_x * 2 + to_k, 128)], c1.at[k, x], C1, row_of(y, zh, to_k), zl * 4 + to_x)
    keep(con_ref.at[:, cols(x * 2 + k, 128)], c1.at[k, x], C1)
    for d in range(1, 8):
        to_y, to_s = (y + d // 2) % 4, (s + d) % 2
        send(val_ref.at[:, cols(to_y * 2 + to_s, 128)], v1.at[y, s], V1, row_of(to_y, zh, k), (h * 2 + to_s) * 4 + x)
    keep(val_ref.at[:, cols(y * 2 + s, 128)], v1.at[y, s], V1)
    sent(xr.at[0:7, 0], ssem.at[C1])
    sent(xr.at[0:7, 0], ssem.at[V1])

    pl.when(at_start)(lambda: hand_on(first))

    partner = (h * 2 + 1 - s) * 4 + x
    arrived(c1, C1)
    send(c1, cb.at[y, :, s], CZ, row, partner)
    keep(c1, cb.at[y, :, s], C2)
    for d in range(1, 4):
        send(c1, cb.at[y, :, s], C2, row_of((y + d) % 4, zh, k), col)
    arrived(v1, V1)
    for d in range(1, 8):
        to_x, to_k = (x + d // 2) % 4, (k + d) % 2
        send(v1, vb.at[:, k, :, x], V2, row_of(y, zh, to_k), zl * 4 + to_x)
    keep(v1, vb.at[:, k, :, x], V2)
    pl.when(jnp.logical_not(at_start))(lambda: hand_on(first))
    arrived(c1, CZ)
    for d in range(1, 4):
        send(cb.at[y, :, 1 - s], cb.at[y, :, 1 - s], C2, row_of((y + d) % 4, zh, k), col)
    hand_on(1 - first)
    sent(c1, ssem.at[CZ])
    sent(vt.at[:, 0:96], ssem.at[C2])
    sent(vt.at[:, 0:112], ssem.at[V2])

    w_hi, w_lo = halves(w_ref[...])
    wh[...] = w_hi
    wl[...] = w_lo

    lane = lax.broadcasted_iota(jnp.int32, (4, 16, 128), 2)
    parts = []
    for v in range(4):
        one, two = xr[v * 2], xr[v * 2 + 1]
        parts.append(jnp.where(lane < 64, one, pltpu.roll(two, 64, 2)))
        parts.append(jnp.where(lane < 64, pltpu.roll(one, 64, 2), two))
    trial = jnp.concatenate([p[:, None] for p in parts], axis=1).reshape(512, 128)
    trial = halves(trial)
    arrived(vt.at[:, 0:112], C2)
    arrived(vb, V2)
    for blk in range(4):
        c_hi, c_lo = halves(cb[blk].reshape(256, 128))
        ch[blk] = c_hi
        cl[blk] = c_lo
        v_t = vb[blk].reshape(256, 128).T
        vt[blk] = v_t
        through = dot3(trial, (c_hi, c_lo), NT).reshape(4, 128, 256)
        dens = jnp.sum(through * v_t[None], axis=1)
        dpart[blk] = jnp.concatenate([dens[:, :128], dens[:, 128:]], axis=0)

    for d in range(1, 8):
        to_x, to_k = (x + d // 2) % 4, (k + d) % 2
        send(dpart.at[to_x], da.at[x * 2 + k], DA, row_of(y, zh, to_k), zl * 4 + to_x)
    keep(dpart.at[x], da.at[x * 2 + k], DA)
    sent(da.at[0:7], ssem.at[DA])
    arrived(da, DA)
    das[...] = jnp.sum(da[...], axis=0)
    for d in range(1, 8):
        to_y, to_s = (y + d // 2) % 4, (s + d) % 2
        send(das, db.at[y * 2 + s], DB, row_of(to_y, zh, k), (h * 2 + to_s) * 4 + x)
    keep(das, db.at[y * 2 + s], DB)
    sent(db.at[0:7], ssem.at[DB])
    arrived(db, DB)
    dbs[...] = jnp.sum(db[...], axis=0)

    for e in range(2):
        send_or_keep(dbs, dw.at[h], rsem.at[DW], selfsem.at[1 + e], density_peer(e))
    arrived(dw, DW)
    d0, d1 = dw[0], dw[1]
    dens = jnp.concatenate([d0[0:4], d1[0:4], d0[4:8], d1[4:8]], axis=1)
    dens = jnp.concatenate([dens, dens], axis=0)
    scr = dot3(halves(dens), (wh[...], wl[...]), NT)
    sp[...] = jnp.concatenate([scr[0:4, :128], scr[0:4, 128:]], axis=0)

    for d in range(1, 16):
        send(sp, sa.at[col], SA, row, (col + d) % 16)
    keep(sp, sa.at[col], SA)
    sent(sa.at[0:15], ssem.at[SA])
    arrived(sa, SA)
    sas[...] = jnp.sum(sa[...], axis=0)
    for d in range(1, 8):
        to_y, to_k = (y + d // 2) % 4, (k + d) % 2
        send(sas, sb.at[y * 2 + k], SB, row_of(to_y, zh, to_k), col)
    keep(sas, sb.at[y * 2 + k], SB)
    sent(sb.at[0:7], ssem.at[SB])
    arrived(sb, SB)

    acc = jnp.zeros((512, 128), F32)
    for blk in range(4):
        pots = []
        for kk in range(2):
            tile = sb[blk * 2 + kk]
            pots.append(jnp.where(h == 0, tile[0:4], tile[4:8]))
        pot = jnp.concatenate(pots, axis=1)
        weighted = (vt[blk][None] * pot[:, None, :]).reshape(512, 256)
        acc = acc + dot3(halves(weighted), (ch[blk], cl[blk]), NN)
    acc = acc.reshape(4, 8, 16, 128)
    for v in range(4):
        one, two = acc[:, v * 2], acc[:, v * 2 + 1]
        kp[v * 2] = jnp.where(lane < 64, one, pltpu.roll(two, 64, 2))
        kp[v * 2 + 1] = jnp.where(lane < 64, pltpu.roll(one, 64, 2), two)

    away = (s * 8 + x - zh * 4 - zl + 33) % 16
    far = jnp.where(away < 7, 1, 0)
    group = zh * 2 + h
    for half in (far, 1 - far):
        for j in (1, 2, 3, 0):
            slot = half * 4 + (k * 2 + x % 2 + j) % 4
            to = pair_peer(slot)
            if half is far or j:
                send(kp.at[slot], kr.at[group], KD, *to)
            else:
                send_or_keep(kp.at[slot], kr.at[group], rsem.at[KD], selfsem.at[3], to)
    sent(kr.at[0:7], ssem.at[KD])
    arrived(kr, KD)
    total = jnp.sum(kr[...], axis=0)
    out_ref[:, 0:16, :] = total[:, :, :64]
    out_ref[:, 16:32, :] = total[:, :, 64:]

    for wait in leaving:
        wait()


def per_device(x_pairs, eps_val, eps_con, orb_val, orb_con, screened_w):
    vmem = pl.BlockSpec(memory_space=pltpu.VMEM)
    kern = pl.pallas_call(
        kernel,
        out_shape=jax.ShapeDtypeStruct((4, 32, 64), F32),
        in_specs=[vmem] * 4,
        out_specs=vmem,
        scratch_shapes=[
            pltpu.VMEM((4, 16, 128), F32),
            pltpu.VMEM((8, 4, 16, 128), F32),
            pltpu.VMEM((4, 2, 16, 128), F32),
            pltpu.VMEM((2, 4, 16, 128), F32),
            pltpu.VMEM((4, 2, 2, 4, 16, 128), F32),
            pltpu.VMEM((4, 2, 2, 4, 16, 128), F32),
            pltpu.VMEM((4, 128, 256), F32),
            pltpu.VMEM((4, 256, 128), BF16),
            pltpu.VMEM((4, 256, 128), BF16),
            pltpu.VMEM((256, 512), BF16),
            pltpu.VMEM((256, 512), BF16),
            pltpu.VMEM((4, 8, 128), F32),
            pltpu.VMEM((8, 8, 128), F32),
            pltpu.VMEM((8, 128), F32),
            pltpu.VMEM((8, 8, 128), F32),
            pltpu.VMEM((8, 128), F32),
            pltpu.VMEM((2, 8, 128), F32),
            pltpu.VMEM((8, 128), F32),
            pltpu.VMEM((16, 8, 128), F32),
            pltpu.VMEM((8, 128), F32),
            pltpu.VMEM((8, 8, 128), F32),
            pltpu.VMEM((8, 4, 16, 128), F32),
            pltpu.VMEM((8, 4, 16, 128), F32),
            pltpu.SemaphoreType.DMA((NSEM,)),
            pltpu.SemaphoreType.DMA((NSEM,)),
            pltpu.SemaphoreType.DMA((4,)),
            pltpu.SemaphoreType.DMA((8,)),
            pltpu.SemaphoreType.DMA((2, 8)),
        ],
        compiler_params=pltpu.CompilerParams(has_side_effects=True, collective_id=0),
        name="bse_apply",
    )(x_pairs, orb_val, orb_con, screened_w)
    diff = eps_con[None, None, :] - eps_val[None, :, None]
    return diff * x_pairs + kern


def solution(mesh):
    in_specs = (
        P(None, "rowpt", "colpt"),
        P("rowpt"),
        P("colpt"),
        P(("rowpt", "colpt"), None),
        P(("rowpt", "colpt"), None),
        P("rowpt", "colpt"),
    )
    out_specs = P(None, "rowpt", "colpt")
    return jax.shard_map(
        per_device, mesh=mesh, in_specs=in_specs, out_specs=out_specs, check_vma=False
    )
```

time: 104 us -> 86.1 us (0.83)
  Pallas kernels: 101 us -> 83.7 us
    pallas_call x1, Pallas kernels: 101 us -> 83.7 us  [per_device(): pl.pallas_call(kernel, out_shape=jax.ShapeDtypeStruct((4, 32, 64), F32),...]
where the time goes in v2:
time: 86.1 us; the launch traced here: 85.9 us
  Pallas kernels  83.7 us (97%)
  other arithmetic  2.22 us (3%)
    pallas_call x1, Pallas kernels, per_device(): pl.pallas_call(kernel, out_shape=jax.ShapeDtypeStruct((4, 32, 64), F32),...  83.7 us

profile of v2, /device:TPU:1, one launch (start us, length us, event | category | flops | bytes accessed | tf_op | source)
XLA Modules:
  0.0 85.9 jit_solution(14621338603534975420)
XLA Ops:
  0.0 0.7 broadcast_subtract_fusion
  0.7 0.0 copy-start
  0.7 83.7 %bse_apply.1 = f32[4,32,64]{2,1,0:T(8,128)} custom-call(f32[4,32,64]{2,1,0:T(8,128)} %x_ref.1, f32[16,1024]{1,0:T(8,128)} %val_ref.1, f32[16,1024]{1,0:T(8,128)} %con_ref.1, f32[256,512]{1,0:T(8,128)} %w_ref.1), custom_call_target="tpu_custom_call" | custom-call | tf_op jit(solution)/shard_map/bse_apply/pallas_call | solution.py:281
  84.4 0.0 copy-done
  84.4 1.5 %multiply_add_fusion = f32[4,32,64]{2,1,0:T(8,128)} fusion(f32[4,32,64]{2,1,0:T(8,128)} %bse_apply.1, f32[4,32,64]{2,1,0:T(8,128)S(1)} %copy-done, f32[32,64]{1,0:T(8,128)S(1)} %broadcast_subtract_fusion), kind=kLoop, calls=%fused_computation | loop fusion | flops 16384 | bytes 106496 | tf_op jit(solution)/shard_map/add | solution.py:320
Async XLA Ops:
  0.7 83.7 %copy-start = (f32[4,32,64]{2,1,0:T(8,128)S(1)}, f32[4,32,64]{2,1,0:T(8,128)}, u32[]{:S(2)}) copy-start(f32[4,32,64]{2,1,0:T(8,128)} %x_ref.1) | copy-start | bytes 98308

commit v3 on v2

v3 whole, which is shorter than its diff:
```python
import jax
import jax.numpy as jnp
from jax import lax
from jax.experimental import pallas as pl
from jax.experimental.pallas import tpu as pltpu
from jax.sharding import PartitionSpec as P

MESH = pl.DeviceIdType.MESH
F32 = jnp.float32
BF16 = jnp.bfloat16

V1, C1, V2, C2, V3, C3, V4, C4, DA, DB, DW, SA, SB, KD = range(14)
NSEM = 14


def halves(a):
    hi = a.astype(BF16)
    return hi, (a - hi.astype(F32)).astype(BF16)


def dot_of(a, b, dims):
    return lax.dot_general(a, b, (dims, ((), ())), preferred_element_type=F32)


def dot3(a, b, dims):
    (ah, al), (bh, bl) = a, b
    return dot_of(ah, bh, dims) + (dot_of(ah, bl, dims) + dot_of(al, bh, dims))


NT = ((1,), (1,))
NN = ((1,), (0,))


def kernel(
    x_ref, ev_ref, ec_ref, val_ref, con_ref, w_ref, out_ref,
    xv, wv, xp, xr, vb, cb, vb2, cb2, vt, ch, cl, wh, wl,
    dpart, da, das, db, dbs, dw, sp, sa, sas, sb, kp, kr,
    rsem, ssem, selfsem, xsem, xout, lsem, ready,
):
    row = lax.axis_index("rowpt")
    col = lax.axis_index("colpt")
    y, zh, k = row // 8, (row // 2) % 4, row % 2
    zl, x = col // 4, col % 4
    s, h = zl % 2, zl // 2

    def row_of(y_, zh_, k_):
        return y_ * 8 + zh_ * 2 + k_

    def send(src, dst, sem, to_row, to_col):
        pltpu.make_async_remote_copy(
            src_ref=src, dst_ref=dst, send_sem=ssem.at[sem], recv_sem=rsem.at[sem],
            device_id=(to_row, to_col), device_id_type=MESH,
        ).start()

    def keep(src, dst, sem):
        pltpu.make_async_copy(src, dst, rsem.at[sem]).start()

    def arrived(buf, sem):
        pltpu.make_async_copy(buf, buf, rsem.at[sem]).wait()

    leaving = []

    def sent(buf, sem, only=None):
        def wait():
            pltpu.make_async_copy(buf, buf, sem).wait()

        leaving.append(wait if only is None else lambda: pl.when(only)(wait))

    def cols(block, width):
        return pl.ds(pl.multiple_of(block * width, width), width)

    def send_or_keep(src, dst, sem, own_sem, to):
        same = (to[0] == row) & (to[1] == col)

        @pl.when(same)
        def _():
            pltpu.make_async_copy(src, dst, sem).start()

        @pl.when(jnp.logical_not(same))
        def _():
            pltpu.make_async_remote_copy(
                src_ref=src, dst_ref=dst, send_sem=own_sem, recv_sem=sem,
                device_id=to, device_id_type=MESH,
            ).start()

        sent(src, own_sem, jnp.logical_not(same))

    xslot = (zh % 2) * 4 + k * 2 + x % 2

    def ring_peer(d):
        to = (zh * 2 + h + d) % 8
        return row_of(y, to // 2, k), ((to % 2) * 2 + s) * 4 + x

    def pair_peer(slot):
        return row_of(y, s * 2 + slot // 4, (slot // 2) % 2), x * 4 + k * 2 + slot % 2

    def density_peer(e):
        return row_of(y, s * 2 + e, k), x * 4 + zh

    def group_peer(d):
        to = (zh * 2 + h + d) % 8
        return row_of(y, to // 2, x // 2), ((to % 2) * 2 + zh // 2) * 4 + zl

    def way_of(q):
        return (zh * 2 + h - 4 * s - 2 * q - x // 2 + 16) % 8

    near = []
    for d in range(1, 16):
        near.append((row_of(y, zh, (k + d) % 2), (h * 2 + (s + d // 2) % 2) * 4 + (x + d // 4) % 4))
    for d in range(4, 16):
        near.append((row_of((y + d // 4) % 4, zh, (k + d) % 2), (h * 2 + (s + d // 2) % 2) * 4 + x))
    for d in range(16):
        near.append((row_of(y, zh, d // 8), ((1 - h) * 2 + d // 4 % 2) * 4 + d % 4))
    for d in range(2, 8):
        near.append((row_of((y + d // 2) % 4, zh, k), ((1 - h) * 2 + d % 2) * 4 + x))
    near += [ring_peer(1), ring_peer(-1)]
    barrier = pltpu.get_barrier_semaphore()
    for to in near:
        pl.semaphore_signal(barrier, inc=1, device_id=to, device_id_type=MESH)

    loads = [
        pltpu.make_async_copy(x_ref, xv, lsem.at[0]),
        pltpu.make_async_copy(w_ref, wv, lsem.at[1]),
    ]
    for load in loads:
        load.start()
    pl.semaphore_wait(barrier, len(near))

    def ring_ready(n):
        for d in (1, -1):
            pl.semaphore_signal(ready.at[n], inc=1, device_id=ring_peer(d), device_id_type=MESH)

    ring_ready(0)

    for d in range(1, 16):
        to_x, to_s, to_k = (x + d // 4) % 4, (s + d // 2) % 2, (k + d) % 2
        send(
            con_ref.at[:, cols(to_x * 2 + to_k, 128)], cb.at[y, k, s, x], C1,
            row_of(y, zh, to_k), (h * 2 + to_s) * 4 + to_x,
        )
    keep(con_ref.at[:, cols(x * 2 + k, 128)], cb.at[y, k, s, x], C1)
    for d in range(1, 8):
        to_y, to_s = (y + d // 2) % 4, (s + d) % 2
        send(
            val_ref.at[:, cols(to_y * 2 + to_s, 128)], vb.at[y, k, s, x], V1,
            row_of(to_y, zh, k), (h * 2 + to_s) * 4 + x,
        )
    keep(val_ref.at[:, cols(y * 2 + s, 128)], vb.at[y, k, s, x], V1)
    sent(vt.at[0, 0:120], ssem.at[C1])
    sent(xr.at[0:7, 0], ssem.at[V1])

    loads[0].wait()
    xp[...] = jnp.concatenate([xv[:, 0:16, :], xv[:, 16:32, :]], axis=2)
    pl.semaphore_wait(ready.at[0], 2)
    ring_ready(1)

    pl.semaphore_wait(ready.at[1], 2)
    for on, d in enumerate((2, -2, 1, -1)):
        pltpu.make_async_remote_copy(
            src_ref=xp, dst_ref=xr.at[xslot], send_sem=xout.at[0, on], recv_sem=xsem.at[xslot],
            device_id=group_peer(d), device_id_type=MESH,
        ).start()
        sent(xp, xout.at[0, on])
    send_or_keep(xp, xr.at[xslot], xsem.at[xslot], selfsem.at[0], group_peer(0))

    arrived(cb.at[y], C1)
    for d in (2, 1, 3):
        send(cb.at[y], cb.at[y], C2, row_of((y + d) % 4, zh, k), col)
    mine = vb.at[:, k, :, x]
    arrived(mine, V1)
    for d in (4, 5, 2, 3, 6, 7, 1):
        to_x, to_k = (x + d // 2) % 4, (k + d) % 2
        send(mine, mine, V2, row_of(y, zh, to_k), zl * 4 + to_x)
    sent(cb.at[0:3], ssem.at[C2])
    sent(vt.at[0:4, 0:112], ssem.at[V2])

    def piece_in(slot):
        pltpu.make_async_copy(xr.at[slot], xr.at[slot], xsem.at[slot]).wait()

    relays = way_of(0) % 2 == 0
    half = jnp.where(way_of(0) % 4 == 2, 0, 1)
    ahead = way_of(half) == 2
    step = jnp.where(ahead, 1, -1)
    odd = jnp.where(ahead, 0, 1)

    @pl.when(relays)
    def _():
        for n in range(4):
            slot = half * 4 + (n % 2) * 2 + (odd if n < 2 else 1 - odd)
            piece_in(slot)
            for on, to in enumerate((2 * step, step)):
                if on or n < 2:
                    pltpu.make_async_remote_copy(
                        src_ref=xr.at[slot], dst_ref=xr.at[slot], send_sem=xout.at[1 + on, n],
                        recv_sem=xsem.at[slot], device_id=ring_peer(to), device_id_type=MESH,
                    ).start()

    for on in range(2):
        for n in range(4):
            if on or n < 2:
                sent(xp, xout.at[1 + on, n], relays)

    @pl.when(jnp.logical_not(relays))
    def _():
        for n in range(4):
            piece_in(half * 4 + n)

    loads[1].wait()
    w_hi, w_lo = halves(wv[...])
    wh[...] = w_hi
    wl[...] = w_lo

    for n in range(4):
        piece_in((1 - half) * 4 + n)

    for d in range(16):
        to_x, to_s, to_k = (x + d // 4) % 4, d // 2 % 2, d % 2
        send(
            con_ref.at[:, cols(to_x * 2 + to_k, 128)], cb2.at[y, k, s, x], C3,
            row_of(y, zh, to_k), ((1 - h) * 2 + to_s) * 4 + to_x,
        )
    for d in range(8):
        to_y, to_s = (y + d // 2) % 4, d % 2
        send(
            val_ref.at[:, cols(to_y * 2 + to_s, 128)], vb2.at[y, k, s, x], V3,
            row_of(to_y, zh, k), ((1 - h) * 2 + to_s) * 4 + x,
        )
    sent(cb2.at[0], ssem.at[C3])
    sent(vb2.at[0, 0], ssem.at[V3])

    lane = lax.broadcasted_iota(jnp.int32, (4, 16, 128), 2)
    parts = []
    for v in range(4):
        one, two = xr[v * 2], xr[v * 2 + 1]
        parts.append(jnp.where(lane < 64, one, pltpu.roll(two, 64, 2)))
        parts.append(jnp.where(lane < 64, pltpu.roll(one, 64, 2), two))
    trial = jnp.concatenate([p[:, None] for p in parts], axis=1).reshape(512, 128)
    trial = halves(trial)
    arrived(cb.at[0:3], C2)
    arrived(vt.at[0:4, 0:112], V2)
    for blk in range(4):
        c_hi, c_lo = halves(cb[blk].reshape(256, 128))
        ch[blk] = c_hi
        cl[blk] = c_lo
        v_t = vb[blk].reshape(256, 128).T
        vt[blk] = v_t
        through = dot3(trial, (c_hi, c_lo), NT).reshape(4, 128, 256)
        dens = jnp.sum(through * v_t[None], axis=1)
        dpart[blk] = jnp.concatenate([dens[:, :128], dens[:, 128:]], axis=0)

    for d in range(1, 8):
        to_x, to_k = (x + d // 2) % 4, (k + d) % 2
        send(dpart.at[to_x], da.at[x * 2 + k], DA, row_of(y, zh, to_k), zl * 4 + to_x)
    keep(dpart.at[x], da.at[x * 2 + k], DA)
    sent(da.at[0:7], ssem.at[DA])
    arrived(da, DA)
    das[...] = jnp.sum(da[...], axis=0)
    for d in range(1, 8):
        to_y, to_s = (y + d // 2) % 4, (s + d) % 2
        send(das, db.at[y * 2 + s], DB, row_of(to_y, zh, k), (h * 2 + to_s) * 4 + x)
    keep(das, db.at[y * 2 + s], DB)
    sent(db.at[0:7], ssem.at[DB])
    arrived(cb2.at[y], C3)
    for d in (2, 1, 3):
        send(cb2.at[y], cb2.at[y], C4, row_of((y + d) % 4, zh, k), col)
    theirs = vb2.at[:, k, :, x]
    arrived(theirs, V3)
    for d in (4, 5, 2, 3, 6, 7, 1):
        to_x, to_k = (x + d // 2) % 4, (k + d) % 2
        send(theirs, theirs, V4, row_of(y, zh, to_k), zl * 4 + to_x)
    sent(cb2.at[0:3], ssem.at[C4])
    sent(vt.at[0:4, 0:112], ssem.at[V4])
    arrived(db, DB)
    dbs[...] = jnp.sum(db[...], axis=0)

    for e in range(2):
        send_or_keep(dbs, dw.at[h], rsem.at[DW], selfsem.at[1 + e], density_peer(e))
    arrived(dw, DW)
    d0, d1 = dw[0], dw[1]
    dens = jnp.concatenate([d0[0:4], d1[0:4], d0[4:8], d1[4:8]], axis=1)
    dens = jnp.concatenate([dens, dens], axis=0)
    scr = dot3(halves(dens), (wh[...], wl[...]), NT)
    sp[...] = jnp.concatenate([scr[0:4, :128], scr[0:4, 128:]], axis=0)

    for d in range(1, 16):
        send(sp, sa.at[col], SA, row, (col + d) % 16)
    keep(sp, sa.at[col], SA)
    sent(sa.at[0:15], ssem.at[SA])
    arrived(cb2.at[0:3], C4)
    arrived(vt.at[0:4, 0:112], V4)
    for blk in range(4):
        ch[4 + blk], cl[4 + blk] = halves(cb2[blk].reshape(256, 128))
        vt[4 + blk] = vb2[blk].reshape(256, 128).T
    arrived(sa, SA)
    sas[...] = jnp.sum(sa[...], axis=0)
    for d in range(1, 8):
        to_y, to_k = (y + d // 2) % 4, (k + d) % 2
        send(sas, sb.at[y * 2 + k], SB, row_of(to_y, zh, to_k), col)
    keep(sas, sb.at[y * 2 + k], SB)
    sent(sb.at[0:7], ssem.at[SB])
    arrived(sb, SB)

    acc = jnp.zeros((512, 128), F32)
    for blk in range(8):
        pots = []
        for kk in range(2):
            tile = sb[blk % 4 * 2 + kk]
            pots.append(jnp.where((h == 0) == (blk < 4), tile[0:4], tile[4:8]))
        pot = jnp.concatenate(pots, axis=1)
        weighted = (vt[blk][None] * pot[:, None, :]).reshape(512, 256)
        acc = acc + dot3(halves(weighted), (ch[blk], cl[blk]), NN)
    acc = acc.reshape(4, 8, 16, 128)
    for v in range(4):
        one, two = acc[:, v * 2], acc[:, v * 2 + 1]
        low = jnp.where(lane < 64, one, pltpu.roll(two, 64, 2))
        high = jnp.where(lane < 64, pltpu.roll(one, 64, 2), two)
        kp[v] = jnp.where(h == 0, low, high)

    away = (s * 8 + x - zh * 4 - zl + 33) % 16
    far = jnp.where(away < 7, 1, 0)
    for hold in (far, 1 - far):
        for j in (1, 0):
            slot = hold * 2 + (k + j) % 2
            to = pair_peer(slot * 2 + h)
            if hold is far or j:
                send(kp.at[slot], kr.at[zh], KD, *to)
            else:
                send_or_keep(kp.at[slot], kr.at[zh], rsem.at[KD], selfsem.at[3], to)
    sent(kr.at[0:3], ssem.at[KD])
    arrived(kr, KD)
    total = jnp.sum(kr[...], axis=0)
    eye = lax.broadcasted_iota(jnp.int32, (32, 32), 0) == lax.broadcasted_iota(jnp.int32, (32, 32), 1)
    ev = jnp.sum(jnp.where(eye, ev_ref[...], 0.0), axis=1, keepdims=True)
    diff = ec_ref[...] - ev
    out_ref[:, 0:16, :] = diff[None, 0:16] * xv[:, 0:16, :] + total[:, :, :64]
    out_ref[:, 16:32, :] = diff[None, 16:32] * xv[:, 16:32, :] + total[:, :, 64:]

    for wait in leaving:
        wait()


def per_device(x_pairs, eps_val, eps_con, orb_val, orb_con, screened_w):
    vmem = pl.BlockSpec(memory_space=pltpu.VMEM)
    anywhere = pl.BlockSpec(memory_space=pl.ANY)
    return pl.pallas_call(
        kernel,
        out_shape=jax.ShapeDtypeStruct((4, 32, 64), F32),
        in_specs=[anywhere, vmem, vmem, anywhere, anywhere, anywhere],
        out_specs=vmem,
        scratch_shapes=[
            pltpu.VMEM((4, 32, 64), F32),
            pltpu.VMEM((256, 512), F32),
            pltpu.VMEM((4, 16, 128), F32),
            pltpu.VMEM((8, 4, 16, 128), F32),
            pltpu.VMEM((4, 2, 2, 4, 16, 128), F32),
            pltpu.VMEM((4, 2, 2, 4, 16, 128), F32),
            pltpu.VMEM((4, 2, 2, 4, 16, 128), F32),
            pltpu.VMEM((4, 2, 2, 4, 16, 128), F32),
            pltpu.VMEM((8, 128, 256), F32),
            pltpu.VMEM((8, 256, 128), BF16),
            pltpu.VMEM((8, 256, 128), BF16),
            pltpu.VMEM((256, 512), BF16),
            pltpu.VMEM((256, 512), BF16),
            pltpu.VMEM((4, 8, 128), F32),
            pltpu.VMEM((8, 8, 128), F32),
            pltpu.VMEM((8, 128), F32),
            pltpu.VMEM((8, 8, 128), F32),
            pltpu.VMEM((8, 128), F32),
            pltpu.VMEM((2, 8, 128), F32),
            pltpu.VMEM((8, 128), F32),
            pltpu.VMEM((16, 8, 128), F32),
            pltpu.VMEM((8, 128), F32),
            pltpu.VMEM((8, 8, 128), F32),
            pltpu.VMEM((4, 4, 16, 128), F32),
            pltpu.VMEM((4, 4, 16, 128), F32),
            pltpu.SemaphoreType.DMA((NSEM,)),
            pltpu.SemaphoreType.DMA((NSEM,)),
            pltpu.SemaphoreType.DMA((4,)),
            pltpu.SemaphoreType.DMA((8,)),
            pltpu.SemaphoreType.DMA((3, 4)),
            pltpu.SemaphoreType.DMA((2,)),
            pltpu.SemaphoreType.REGULAR((2,)),
        ],
        compiler_params=pltpu.CompilerParams(has_side_effects=True, collective_id=0),
        name="bse_apply",
    )(x_pairs, eps_val[None], eps_con[None], orb_val, orb_con, screened_w)


def solution(mesh):
    in_specs = (
        P(None, "rowpt", "colpt"),
        P("rowpt"),
        P("colpt"),
        P(("rowpt", "colpt"), None),
        P(("rowpt", "colpt"), None),
        P("rowpt", "colpt"),
    )
    out_specs = P(None, "rowpt", "colpt")
    return jax.shard_map(
        per_device, mesh=mesh, in_specs=in_specs, out_specs=out_specs, check_vma=False
    )
```

time: 86.1 us -> 78.7 us (0.914)
  the two profiles are of different devices: /device:TPU:1 before, /device:TPU:96 now
where the time goes in v3:
time: 78.7 us; the launch traced here: 78.6 us
  Pallas kernels  77.1 us (98%)
  local copies, waits for them, and re-layouts  1.47 us (2%)
    pallas_call x1, Pallas kernels, per_device(): pl.pallas_call(kernel, out_shape=jax.ShapeDtypeStruct((4, 32, 64), F32),...  77.1 us

profile of v3, /device:TPU:96, one launch (start us, length us, event | category | flops | bytes accessed | tf_op | source)
XLA Modules:
  0.0 78.6 jit_solution(8977510343960953086)
XLA Ops:
  0.0 77.1 %bse_apply.1 = f32[4,32,64]{2,1,0:T(8,128)} custom-call(f32[4,32,64]{2,1,0:T(8,128)} %x_ref.1, f32[1,32]{1,0:T(1,128)} %bitcast.2, f32[1,64]{1,0:T(1,128)} %bitcast.3, f32[16,1024]{1,0:T(8,128)} %val_ref.1, f32[16,1024]{1,0:T(8,128)} %con_ref.1, f32[256,512]{1,0:T(8,128)} %w_ref.1), custom_call_target="tpu_custom_call" | custom-call | tf_op jit(solution)/shard_map/bse_apply/pallas_call | solution.py:345
  77.1 1.5 %copy.8 = f32[4,32,64]{2,1,0:T(8,128)} copy(f32[4,32,64]{2,1,0:T(8,128)} %bse_apply.1) | data formatting | bytes 65536

commit v4 on v3

--- a/solution.py
+++ b/solution.py
@@ -35,7 +35,7 @@
     x_ref, ev_ref, ec_ref, val_ref, con_ref, w_ref, out_ref,
     xv, wv, xp, xr, vb, cb, vb2, cb2, vt, ch, cl, wh, wl,
     dpart, da, das, db, dbs, dw, sp, sa, sas, sb, kp, kr,
-    rsem, ssem, selfsem, xsem, xout, lsem, ready,
+    rsem, ssem, selfsem, xsem, xout, lsem,
 ):
     row = lax.axis_index("rowpt")
     col = lax.axis_index("colpt")
@@ -69,6 +69,9 @@
     def cols(block, width):
         return pl.ds(pl.multiple_of(block * width, width), width)
 
+    def con_cols(x_, k_):
+        return cols((k_ * 2 + x_ % 2) * 2 + x_ // 2, 128)
+
     def send_or_keep(src, dst, sem, own_sem, to):
         same = (to[0] == row) & (to[1] == col)
 
@@ -92,17 +95,17 @@
         return row_of(y, to // 2, k), ((to % 2) * 2 + s) * 4 + x
 
     def pair_peer(slot):
-        return row_of(y, s * 2 + slot // 4, (slot // 2) % 2), x * 4 + k * 2 + slot % 2
+        return row_of(y, s * 2 + slot // 4, (slot // 2) % 2), (k * 2 + x % 2) * 4 + x // 2 * 2 + slot % 2
 
     def density_peer(e):
         return row_of(y, s * 2 + e, k), x * 4 + zh
 
     def group_peer(d):
         to = (zh * 2 + h + d) % 8
-        return row_of(y, to // 2, x // 2), ((to % 2) * 2 + zh // 2) * 4 + zl
+        return row_of(y, to // 2, zl // 2), ((to % 2) * 2 + zh // 2) * 4 + x // 2 * 2 + zl % 2
 
     def way_of(q):
-        return (zh * 2 + h - 4 * s - 2 * q - x // 2 + 16) % 8
+        return (zh * 2 + h - 4 * s - 2 * q - k + 16) % 8
 
     near = []
     for d in range(1, 16):
@@ -113,8 +116,19 @@
         near.append((row_of(y, zh, d // 8), ((1 - h) * 2 + d // 4 % 2) * 4 + d % 4))
     for d in range(2, 8):
         near.append((row_of((y + d // 2) % 4, zh, k), ((1 - h) * 2 + d % 2) * 4 + x))
-    near += [ring_peer(1), ring_peer(-1)]
+    for d in (1, -1, 2, -2):
+        near += [ring_peer(d), group_peer(d)]
     barrier = pltpu.get_barrier_semaphore()
+    expected = len(near)
+    for q in range(2):
+        direct = jnp.where((way_of(q) + 2) % 8 < 5, 1, 0) - jnp.where(way_of(q) == 0, 1, 0)
+        expected = expected + 4 * direct
+
+        @pl.when(direct == 1)
+        def _():
+            for j in range(4):
+                pl.semaphore_signal(barrier, inc=1, device_id=pair_peer(q * 4 + j), device_id_type=MESH)
+
     for to in near:
         pl.semaphore_signal(barrier, inc=1, device_id=to, device_id_type=MESH)
 
@@ -124,21 +138,16 @@
     ]
     for load in loads:
         load.start()
-    pl.semaphore_wait(barrier, len(near))
-
-    def ring_ready(n):
-        for d in (1, -1):
-            pl.semaphore_signal(ready.at[n], inc=1, device_id=ring_peer(d), device_id_type=MESH)
-
-    ring_ready(0)
+    pl.semaphore_wait(barrier, expected)
+
 
     for d in range(1, 16):
         to_x, to_s, to_k = (x + d // 4) % 4, (s + d // 2) % 2, (k + d) % 2
         send(
-            con_ref.at[:, cols(to_x * 2 + to_k, 128)], cb.at[y, k, s, x], C1,
+            con_ref.at[:, con_cols(to_x, to_k)], cb.at[y, k, s, x], C1,
             row_of(y, zh, to_k), (h * 2 + to_s) * 4 + to_x,
         )
-    keep(con_ref.at[:, cols(x * 2 + k, 128)], cb.at[y, k, s, x], C1)
+    keep(con_ref.at[:, con_cols(x, k)], cb.at[y, k, s, x], C1)
     for d in range(1, 8):
         to_y, to_s = (y + d // 2) % 4, (s + d) % 2
         send(
@@ -151,10 +160,7 @@
 
     loads[0].wait()
     xp[...] = jnp.concatenate([xv[:, 0:16, :], xv[:, 16:32, :]], axis=2)
-    pl.semaphore_wait(ready.at[0], 2)
-    ring_ready(1)
-
-    pl.semaphore_wait(ready.at[1], 2)
+
     for on, d in enumerate((2, -2, 1, -1)):
         pltpu.make_async_remote_copy(
             src_ref=xp, dst_ref=xr.at[xslot], send_sem=xout.at[0, on], recv_sem=xsem.at[xslot],
@@ -216,7 +222,7 @@
     for d in range(16):
         to_x, to_s, to_k = (x + d // 4) % 4, d // 2 % 2, d % 2
         send(
-            con_ref.at[:, cols(to_x * 2 + to_k, 128)], cb2.at[y, k, s, x], C3,
+            con_ref.at[:, con_cols(to_x, to_k)], cb2.at[y, k, s, x], C3,
             row_of(y, zh, to_k), ((1 - h) * 2 + to_s) * 4 + to_x,
         )
     for d in range(8):
@@ -260,6 +266,11 @@
         send(das, db.at[y * 2 + s], DB, row_of(to_y, zh, k), (h * 2 + to_s) * 4 + x)
     keep(das, db.at[y * 2 + s], DB)
     sent(db.at[0:7], ssem.at[DB])
+    arrived(db, DB)
+    dbs[...] = jnp.sum(db[...], axis=0)
+
+    for e in range(2):
+        send_or_keep(dbs, dw.at[h], rsem.at[DW], selfsem.at[1 + e], density_peer(e))
     arrived(cb2.at[y], C3)
     for d in (2, 1, 3):
         send(cb2.at[y], cb2.at[y], C4, row_of((y + d) % 4, zh, k), col)
@@ -270,11 +281,6 @@
         send(theirs, theirs, V4, row_of(y, zh, to_k), zl * 4 + to_x)
     sent(cb2.at[0:3], ssem.at[C4])
     sent(vt.at[0:4, 0:112], ssem.at[V4])
-    arrived(db, DB)
-    dbs[...] = jnp.sum(db[...], axis=0)
-
-    for e in range(2):
-        send_or_keep(dbs, dw.at[h], rsem.at[DW], selfsem.at[1 + e], density_peer(e))
     arrived(dw, DW)
     d0, d1 = dw[0], dw[1]
     dens = jnp.concatenate([d0[0:4], d1[0:4], d0[4:8], d1[4:8]], axis=1)
@@ -316,7 +322,7 @@
         high = jnp.where(lane < 64, pltpu.roll(one, 64, 2), two)
         kp[v] = jnp.where(h == 0, low, high)
 
-    away = (s * 8 + x - zh * 4 - zl + 33) % 16
+    away = (s * 8 + k * 2 + x % 2 - zh * 4 - zl + 33) % 16
     far = jnp.where(away < 7, 1, 0)
     for hold in (far, 1 - far):
         for j in (1, 0):
@@ -379,7 +385,6 @@
             pltpu.SemaphoreType.DMA((8,)),
             pltpu.SemaphoreType.DMA((3, 4)),
             pltpu.SemaphoreType.DMA((2,)),
-            pltpu.SemaphoreType.REGULAR((2,)),
         ],
         compiler_params=pltpu.CompilerParams(has_side_effects=True, collective_id=0),
         name="bse_apply",

time: 78.7 us -> 75.8 us (0.963)
  the two profiles are of different devices: /device:TPU:96 before, /device:TPU:32 now
where the time goes in v4:
time: 75.8 us; the launch traced here: 75.7 us
  Pallas kernels  74.2 us (98%)
  local copies, waits for them, and re-layouts  1.47 us (2%)
    pallas_call x1, Pallas kernels, per_device(): pl.pallas_call(kernel, out_shape=jax.ShapeDtypeStruct((4, 32, 64), F32),...  74.2 us

profile of v4, /device:TPU:32, one launch (start us, length us, event | category | flops | bytes accessed | tf_op | source)
XLA Modules:
  0.0 75.7 jit_solution(15830758352816372116)
XLA Ops:
  0.0 74.2 %bse_apply.1 = f32[4,32,64]{2,1,0:T(8,128)} custom-call(f32[4,32,64]{2,1,0:T(8,128)} %x_ref.1, f32[1,32]{1,0:T(1,128)} %bitcast.2, f32[1,64]{1,0:T(1,128)} %bitcast.3, f32[16,1024]{1,0:T(8,128)} %val_ref.1, f32[16,1024]{1,0:T(8,128)} %con_ref.1, f32[256,512]{1,0:T(8,128)} %w_ref.1), custom_call_target="tpu_custom_call" | custom-call | tf_op jit(solution)/shard_map/bse_apply/pallas_call | solution.py:351
  74.2 1.5 %copy.8 = f32[4,32,64]{2,1,0:T(8,128)} copy(f32[4,32,64]{2,1,0:T(8,128)} %bse_apply.1) | data formatting | bytes 65536

commit v5 on v4

--- a/solution.py
+++ b/solution.py
@@ -35,7 +35,7 @@
     x_ref, ev_ref, ec_ref, val_ref, con_ref, w_ref, out_ref,
     xv, wv, xp, xr, vb, cb, vb2, cb2, vt, ch, cl, wh, wl,
     dpart, da, das, db, dbs, dw, sp, sa, sas, sb, kp, kr,
-    rsem, ssem, selfsem, xsem, xout, lsem,
+    rsem, ssem, selfsem, xsem, xout, lsem, ready,
 ):
     row = lax.axis_index("rowpt")
     col = lax.axis_index("colpt")
@@ -108,16 +108,12 @@
         return (zh * 2 + h - 4 * s - 2 * q - k + 16) % 8
 
     near = []
-    for d in range(1, 16):
+    for d in (2, -2, 1, -1):
+        near += [group_peer(d), ring_peer(d)]
+    for d in (8, 9, 10, 11, 4, 5, 6, 7, 12, 13, 14, 15, 1, 2, 3):
         near.append((row_of(y, zh, (k + d) % 2), (h * 2 + (s + d // 2) % 2) * 4 + (x + d // 4) % 4))
-    for d in range(4, 16):
-        near.append((row_of((y + d // 4) % 4, zh, (k + d) % 2), (h * 2 + (s + d // 2) % 2) * 4 + x))
-    for d in range(16):
-        near.append((row_of(y, zh, d // 8), ((1 - h) * 2 + d // 4 % 2) * 4 + d % 4))
-    for d in range(2, 8):
-        near.append((row_of((y + d // 2) % 4, zh, k), ((1 - h) * 2 + d % 2) * 4 + x))
-    for d in (1, -1, 2, -2):
-        near += [ring_peer(d), group_peer(d)]
+    for d in (4, 5, 2, 3, 6, 7):
+        near.append((row_of((y + d // 2) % 4, zh, k), (h * 2 + (s + d) % 2) * 4 + x))
     barrier = pltpu.get_barrier_semaphore()
     expected = len(near)
     for q in range(2):
@@ -139,6 +135,7 @@
     for load in loads:
         load.start()
     pl.semaphore_wait(barrier, expected)
+    pl.semaphore_signal(ready.at[0], inc=1, device_id=ring_peer(1 - 2 * h), device_id_type=MESH)
 
 
     for d in range(1, 16):
@@ -218,21 +215,6 @@
 
     for n in range(4):
         piece_in((1 - half) * 4 + n)
-
-    for d in range(16):
-        to_x, to_s, to_k = (x + d // 4) % 4, d // 2 % 2, d % 2
-        send(
-            con_ref.at[:, con_cols(to_x, to_k)], cb2.at[y, k, s, x], C3,
-            row_of(y, zh, to_k), ((1 - h) * 2 + to_s) * 4 + to_x,
-        )
-    for d in range(8):
-        to_y, to_s = (y + d // 2) % 4, d % 2
-        send(
-            val_ref.at[:, cols(to_y * 2 + to_s, 128)], vb2.at[y, k, s, x], V3,
-            row_of(to_y, zh, k), ((1 - h) * 2 + to_s) * 4 + x,
-        )
-    sent(cb2.at[0], ssem.at[C3])
-    sent(vb2.at[0, 0], ssem.at[V3])
 
     lane = lax.broadcasted_iota(jnp.int32, (4, 16, 128), 2)
     parts = []
@@ -254,14 +236,29 @@
         dens = jnp.sum(through * v_t[None], axis=1)
         dpart[blk] = jnp.concatenate([dens[:, :128], dens[:, 128:]], axis=0)
 
-    for d in range(1, 8):
+    for d in (4, 5, 2, 3, 6, 7, 1):
         to_x, to_k = (x + d // 2) % 4, (k + d) % 2
         send(dpart.at[to_x], da.at[x * 2 + k], DA, row_of(y, zh, to_k), zl * 4 + to_x)
     keep(dpart.at[x], da.at[x * 2 + k], DA)
     sent(da.at[0:7], ssem.at[DA])
+    pl.semaphore_wait(ready.at[0], 1)
+    for d in range(16):
+        to_x, to_s, to_k = (x + d // 4) % 4, d // 2 % 2, d % 2
+        send(
+            con_ref.at[:, con_cols(to_x, to_k)], cb2.at[y, k, s, x], C3,
+            row_of(y, zh, to_k), ((1 - h) * 2 + to_s) * 4 + to_x,
+        )
+    for d in range(8):
+        to_y, to_s = (y + d // 2) % 4, d % 2
+        send(
+            val_ref.at[:, cols(to_y * 2 + to_s, 128)], vb2.at[y, k, s, x], V3,
+            row_of(to_y, zh, k), ((1 - h) * 2 + to_s) * 4 + x,
+        )
+    sent(cb2.at[0], ssem.at[C3])
+    sent(vb2.at[0, 0], ssem.at[V3])
     arrived(da, DA)
     das[...] = jnp.sum(da[...], axis=0)
-    for d in range(1, 8):
+    for d in (4, 5, 2, 3, 6, 7, 1):
         to_y, to_s = (y + d // 2) % 4, (s + d) % 2
         send(das, db.at[y * 2 + s], DB, row_of(to_y, zh, k), (h * 2 + to_s) * 4 + x)
     keep(das, db.at[y * 2 + s], DB)
@@ -288,7 +285,7 @@
     scr = dot3(halves(dens), (wh[...], wl[...]), NT)
     sp[...] = jnp.concatenate([scr[0:4, :128], scr[0:4, 128:]], axis=0)
 
-    for d in range(1, 16):
+    for d in (10, 6, 14, 8, 9, 11, 12, 13, 4, 5, 7, 15, 2, 1, 3):
         send(sp, sa.at[col], SA, row, (col + d) % 16)
     keep(sp, sa.at[col], SA)
     sent(sa.at[0:15], ssem.at[SA])
@@ -299,32 +296,32 @@
         vt[4 + blk] = vb2[blk].reshape(256, 128).T
     arrived(sa, SA)
     sas[...] = jnp.sum(sa[...], axis=0)
-    for d in range(1, 8):
+    for d in (4, 5, 2, 3, 6, 7, 1):
         to_y, to_k = (y + d // 2) % 4, (k + d) % 2
         send(sas, sb.at[y * 2 + k], SB, row_of(to_y, zh, to_k), col)
     keep(sas, sb.at[y * 2 + k], SB)
     sent(sb.at[0:7], ssem.at[SB])
     arrived(sb, SB)
 
-    acc = jnp.zeros((512, 128), F32)
-    for blk in range(8):
-        pots = []
-        for kk in range(2):
-            tile = sb[blk % 4 * 2 + kk]
-            pots.append(jnp.where((h == 0) == (blk < 4), tile[0:4], tile[4:8]))
-        pot = jnp.concatenate(pots, axis=1)
-        weighted = (vt[blk][None] * pot[:, None, :]).reshape(512, 256)
-        acc = acc + dot3(halves(weighted), (ch[blk], cl[blk]), NN)
-    acc = acc.reshape(4, 8, 16, 128)
-    for v in range(4):
-        one, two = acc[:, v * 2], acc[:, v * 2 + 1]
-        low = jnp.where(lane < 64, one, pltpu.roll(two, 64, 2))
-        high = jnp.where(lane < 64, pltpu.roll(one, 64, 2), two)
-        kp[v] = jnp.where(h == 0, low, high)
-
     away = (s * 8 + k * 2 + x % 2 - zh * 4 - zl + 33) % 16
     far = jnp.where(away < 7, 1, 0)
+    pots = []
+    for blk in range(8):
+        tiles = (sb[blk % 4 * 2], sb[blk % 4 * 2 + 1])
+        pots.append(jnp.concatenate([jnp.where((h == 0) == (blk < 4), t[0:4], t[4:8]) for t in tiles], axis=1))
+    lane = lax.broadcasted_iota(jnp.int32, (4, 16, 128), 2)
     for hold in (far, 1 - far):
+        acc = jnp.zeros((256, 128), F32)
+        for blk in range(8):
+            rows = vt[blk, pl.ds(pl.multiple_of(hold * 64, 64), 64), :]
+            weighted = (rows[None] * pots[blk][:, None, :]).reshape(256, 256)
+            acc = acc + dot3(halves(weighted), (ch[blk], cl[blk]), NN)
+        acc = acc.reshape(4, 4, 16, 128)
+        for v in range(2):
+            one, two = acc[:, v * 2], acc[:, v * 2 + 1]
+            low = jnp.where(lane < 64, one, pltpu.roll(two, 64, 2))
+            high = jnp.where(lane < 64, pltpu.roll(one, 64, 2), two)
+            kp[hold * 2 + v] = jnp.where(h == 0, low, high)
         for j in (1, 0):
             slot = hold * 2 + (k + j) % 2
             to = pair_peer(slot * 2 + h)
@@ -385,6 +382,7 @@
             pltpu.SemaphoreType.DMA((8,)),
             pltpu.SemaphoreType.DMA((3, 4)),
             pltpu.SemaphoreType.DMA((2,)),
+            pltpu.SemaphoreType.REGULAR((1,)),
         ],
         compiler_params=pltpu.CompilerParams(has_side_effects=True, collective_id=0),
         name="bse_apply",

time: 75.8 us -> 70.2 us (0.926)
  the two profiles are of different devices: /device:TPU:32 before, /device:TPU:1 now
where the time goes in v5:
time: 70.2 us; the launch traced here: 70 us
  Pallas kernels  68.5 us (98%)
  local copies, waits for them, and re-layouts  1.47 us (2%)
    pallas_call x1, Pallas kernels, per_device(): pl.pallas_call(kernel, out_shape=jax.ShapeDtypeStruct((4, 32, 64), F32),...  68.5 us
    unnamed x1, local copies, waits for them, and re-layouts  1.47 us

profile of v5, /device:TPU:1, one launch (start us, length us, event | category | flops | bytes accessed | tf_op | source)
XLA Modules:
  0.0 70.0 jit_solution(13567771396379197820)
XLA Ops:
  0.0 68.5 %bse_apply.1 = f32[4,32,64]{2,1,0:T(8,128)} custom-call(f32[4,32,64]{2,1,0:T(8,128)} %x_ref.1, f32[1,32]{1,0:T(1,128)} %bitcast.2, f32[1,64]{1,0:T(1,128)} %bitcast.3, f32[16,1024]{1,0:T(8,128)} %val_ref.1, f32[16,1024]{1,0:T(8,128)} %con_ref.1, f32[256,512]{1,0:T(8,128)} %w_ref.1), custom_call_target="tpu_custom_call" | custom-call | tf_op jit(solution)/shard_map/bse_apply/pallas_call | solution.py:348
  68.5 1.5 %copy.8 = f32[4,32,64]{2,1,0:T(8,128)} copy(f32[4,32,64]{2,1,0:T(8,128)} %bse_apply.1) | data formatting | bytes 65536

commit v6 on v5

--- a/solution.py
+++ b/solution.py
@@ -9,8 +9,8 @@
 F32 = jnp.float32
 BF16 = jnp.bfloat16
 
-V1, C1, V2, C2, V3, C3, V4, C4, DA, DB, DW, SA, SB, KD = range(14)
-NSEM = 14
+V1, C1, V2, C2, V3, C3, V4, C4, C5, DA, DB, DW, SA, SB, KD = range(15)
+NSEM = 15
 
 
 def halves(a):
@@ -141,7 +141,7 @@
     for d in range(1, 16):
         to_x, to_s, to_k = (x + d // 4) % 4, (s + d // 2) % 2, (k + d) % 2
         send(
-            con_ref.at[:, con_cols(to_x, to_k)], cb.at[y, k, s, x], C1,
+            con_ref.at[:, con_cols(to_x, to_k)], cb.at[y, k, s, x], C5 if d // 2 % 2 else C1,
             row_of(y, zh, to_k), (h * 2 + to_s) * 4 + to_x,
         )
     keep(con_ref.at[:, con_cols(x, k)], cb.at[y, k, s, x], C1)
@@ -152,7 +152,8 @@
             row_of(to_y, zh, k), (h * 2 + to_s) * 4 + x,
         )
     keep(val_ref.at[:, cols(y * 2 + s, 128)], vb.at[y, k, s, x], V1)
-    sent(vt.at[0, 0:120], ssem.at[C1])
+    sent(xr.at[0:7, 0], ssem.at[C1])
+    sent(xr.at[0:8, 0], ssem.at[C5])
     sent(xr.at[0:7, 0], ssem.at[V1])
 
     loads[0].wait()
@@ -166,9 +167,10 @@
         sent(xp, xout.at[0, on])
     send_or_keep(xp, xr.at[xslot], xsem.at[xslot], selfsem.at[0], group_peer(0))
 
-    arrived(cb.at[y], C1)
-    for d in (2, 1, 3):
-        send(cb.at[y], cb.at[y], C2, row_of((y + d) % 4, zh, k), col)
+    for sem, part in ((C1, s), (C5, 1 - s)):
+        arrived(cb.at[y, :, part], sem)
+        for d in (2, 1, 3):
+            send(cb.at[y, :, part], cb.at[y, :, part], C2, row_of((y + d) % 4, zh, k), col)
     mine = vb.at[:, k, :, x]
     arrived(mine, V1)
     for d in (4, 5, 2, 3, 6, 7, 1):

time: 70.2 us -> 69.9 us (level)
  no operation moved by 1% of the time
where the time goes in v6:
time: 69.9 us; the launch traced here: 69.7 us
  Pallas kernels  68.2 us (98%)
  local copies, waits for them, and re-layouts  1.47 us (2%)
    pallas_call x1, Pallas kernels, per_device(): pl.pallas_call(kernel, out_shape=jax.ShapeDtypeStruct((4, 32, 64), F32),...  68.2 us
    unnamed x1, local copies, waits for them, and re-layouts  1.47 us

profile of v6, /device:TPU:1, one launch (start us, length us, event | category | flops | bytes accessed | tf_op | source)
XLA Modules:
  0.0 69.7 jit_solution(9760773170851444259)
XLA Ops:
  0.0 68.2 %bse_apply.1 = f32[4,32,64]{2,1,0:T(8,128)} custom-call(f32[4,32,64]{2,1,0:T(8,128)} %x_ref.1, f32[1,32]{1,0:T(1,128)} %bitcast.2, f32[1,64]{1,0:T(1,128)} %bitcast.3, f32[16,1024]{1,0:T(8,128)} %val_ref.1, f32[16,1024]{1,0:T(8,128)} %con_ref.1, f32[256,512]{1,0:T(8,128)} %w_ref.1), custom_call_target="tpu_custom_call" | custom-call | tf_op jit(solution)/shard_map/bse_apply/pallas_call | solution.py:350
  68.2 1.5 %copy.8 = f32[4,32,64]{2,1,0:T(8,128)} copy(f32[4,32,64]{2,1,0:T(8,128)} %bse_apply.1) | data formatting | bytes 65536
